TPU v7x, 32 devices: a whole 2x2x4 slice. The times are simulated.
32 devices in a mesh: group: 4 (over y, x), member: 8 (over z, core).
Axes of the slice: x: 2, y: 2, z: 4, core: 2. Of those that a mesh axis runs over, the one named last changes fastest.
Arguments:
- picture_embedding_matrix: bfloat16 [8192, 1152], P(('group', 'member')), may hold values from -1 to 1
- caption_embedding_matrix: bfloat16 [8192, 1152], P(('group', 'member')), may hold values from -1 to 1
- learned_sharpness: float32 [1], replicated, may hold values from 5 to 20
- learned_offset_entry: float32 [1], replicated, may hold values from -4 to -2
Outputs:
- grad_images: float32 [8192, 1152], P(('group', 'member'))
- grad_texts: float32 [8192, 1152], P(('group', 'member'))
All inputs are finite; a program needn't handle non-finite values.
Results may differ from a plain program's by a relative error of at most 0.002.
Values may be sent and summed in bfloat16 or wider, within the bound.
A program may use at most 192 MiB of HBM per device.

v0:
```python
import jax
import jax.numpy as jnp
from jax import lax
from jax.sharding import PartitionSpec as P


def passed_along(shard, axis, by):
    devices = lax.axis_size(axis)
    return lax.ppermute(shard, axis, [(i, (i + by) % devices) for i in range(devices)])


def weighting_factors(similarity_scores, match_polarity, sharpness_multiplier):
    return (
        -sharpness_multiplier * match_polarity * jax.nn.sigmoid(-match_polarity * similarity_scores)
    ).astype(jnp.bfloat16)


def shards(
    picture_embedding_matrix, caption_embedding_matrix, learned_sharpness, learned_offset_entry
):
    sharpness_multiplier = learned_sharpness[0]
    offset_amount = learned_offset_entry[0]
    count_of_rows = picture_embedding_matrix.shape[0]
    member_idx = lax.axis_index("member")
    members = lax.axis_size("member")
    columns = lax.broadcasted_iota(jnp.int32, (count_of_rows, count_of_rows * members), 1)
    targets = (
        lax.broadcasted_iota(jnp.int32, (count_of_rows, count_of_rows * members), 0)
        + member_idx * count_of_rows
    )
    match_polarity = jnp.where(columns == targets, 1.0, -1.0).astype(jnp.float32)
    txt_prev = passed_along(caption_embedding_matrix, "group", 1)
    earlier_scores = (
        sharpness_multiplier
        * jnp.dot(picture_embedding_matrix, txt_prev.T, preferred_element_type=jnp.float32)
        + offset_amount
    )
    earlier_multipliers = weighting_factors(earlier_scores, -1.0, sharpness_multiplier)
    grad_prev = jnp.dot(earlier_multipliers, txt_prev, preferred_element_type=jnp.float32)
    group_text_rows, group_img = (
        lax.all_gather(caption_embedding_matrix, "member", axis=0, tiled=True),
        lax.all_gather(picture_embedding_matrix, "member", axis=0, tiled=True),
    )
    similarity_scores = (
        sharpness_multiplier
        * jnp.dot(picture_embedding_matrix, group_text_rows.T, preferred_element_type=jnp.float32)
        + offset_amount
    )
    score_multipliers = weighting_factors(similarity_scores, match_polarity, sharpness_multiplier)
    grad_images = (
        jnp.dot(score_multipliers, group_text_rows, preferred_element_type=jnp.float32) + grad_prev
    )
    text_logits = (
        sharpness_multiplier
        * jnp.dot(caption_embedding_matrix, group_img.T, preferred_element_type=jnp.float32)
        + offset_amount
    )
    text_coeffs = weighting_factors(text_logits, match_polarity, sharpness_multiplier)
    img_next = passed_along(picture_embedding_matrix, "group", -1)
    next_logits = (
        sharpness_multiplier
        * jnp.dot(caption_embedding_matrix, img_next.T, preferred_element_type=jnp.float32)
        + offset_amount
    )
    next_coeffs = weighting_factors(next_logits, -1.0, sharpness_multiplier)
    grad_texts = jnp.dot(text_coeffs, group_img, preferred_element_type=jnp.float32)
    grad_texts = grad_texts + jnp.dot(next_coeffs, img_next, preferred_element_type=jnp.float32)
    return (grad_images, grad_texts)


def solution(mesh):
    in_specs = (P(("group", "member"), None), P(("group", "member"), None), P(), P())
    out_specs = (P(("group", "member"), None), P(("group", "member"), None))
    return jax.shard_map(shards, mesh=mesh, in_specs=in_specs, out_specs=out_specs, check_vma=False)
```

profile of v0, /device:TPU:0, one launch (start us, length us, event | category | flops | bytes accessed | tf_op | source)
XLA Modules:
  0.0 134.1 jit_solution(1650488425485670412)
XLA Ops:
  7.2 0.0 all-gather.5.cloned.1.call-start
  7.2 0.7 all-gather.5.cloned.1.call-update
  7.9 0.0 all-gather.3.cloned.1.call-start
  7.9 0.7 all-gather.3.cloned.1.call-update
  8.6 4.0 %collective-permute-start.1 = (bf16[256,1152]{1,0:T(8,128)(2,1)}, bf16[256,1152]{1,0:T(8,128)(2,1)S(1)}, u32[]{:S(2)}, u32[]{:S(2)}) collective-permute-start(bf16[256,1152]{1,0:T(8,128)(2,1)} %param.4), channel_id=1, source_target_pairs={{0,24},{8,0},{16,8},{24,16},{1,25},{9,1},{17,9},{25,17},{2,26},{10... | collective-permute-start | bytes 1769480 | tf_op jit(solution)/shard_map/ppermute | solution.py:9
  12.6 0.0 collective-permute-start
  13.9 49.6 %all-gather.5.cloned.1.call-done = bf16[2048,1152]{1,0:T(8,128)(2,1)} async-done(((bf16[256,1152]{1,0:T(8,128)(2,1)}), bf16[2048,1152]{1,0:T(8,128)(2,1)}) %all-gather.5.cloned.1.call-update) | async-done | bytes 4718608 | tf_op jit(solution)/shard_map/all_gather | solution.py:42
  63.6 0.0 copy-start.1
  63.6 8.1 %fusion.17 = f32[256,1152]{1,0:T(8,128)} fusion(bf16[2048,1152]{1,0:T(8,128)(2,1)} %all-gather.5.cloned.1.call-done, bf16[256,1152]{1,0:T(8,128)(2,1)} %param.5, f32[]{:T(128)} %bitcast.21, f32[]{:T(128)} %bitcast.17, s32[256]{0:T(256)S(1)} %iota_add_fusion, f32[]{:T(128)S(6)} %neg.22), kind=kOutput, calls=%fused_computation.24 | convolution fusion | flops 2422210560 | bytes 6489100 | tf_op jit(solution)/shard_map/dot_general | solution.py:66
  71.7 43.6 %all-gather.3.cloned.1.call-done = bf16[2048,1152]{1,0:T(8,128)(2,1)} async-done(((bf16[256,1152]{1,0:T(8,128)(2,1)}), bf16[2048,1152]{1,0:T(8,128)(2,1)}) %all-gather.3.cloned.1.call-update) | async-done | bytes 4718608 | tf_op jit(solution)/shard_map/all_gather | solution.py:41
  115.2 0.0 copy-done.1
  115.2 0.0 copy-start
  115.2 6.9 %fusion.16 = f32[256,1152]{1,0:T(8,128)S(1)} fusion(bf16[2048,1152]{1,0:T(8,128)(2,1)} %all-gather.3.cloned.1.call-done, bf16[256,1152]{1,0:T(8,128)(2,1)S(1)} %copy-done.1, f32[]{:T(128)} %bitcast.19, f32[]{:T(128)} %bitcast.15, s32[256]{0:T(256)S(1)} %iota_add_fusion, f32[]{:T(128)S(6)} %neg.22), kind=kOutput, calls=%fused_computation.23 | convolution fusion | flops 2422210560 | bytes 6489100 | tf_op jit(solution)/shard_map/dot_general | solution.py:51
  122.1 0.0 collective-permute-done.1
  122.1 0.0 copy-done
  122.1 3.2 %convolution_add_fusion = f32[256,1152]{1,0:T(8,128)} fusion(f32[256,1152]{1,0:T(8,128)} %fusion.17, bf16[256,1152]{1,0:T(8,128)(2,1)S(1)} %collective-permute-done.1, bf16[256,1152]{1,0:T(8,128)(2,1)S(1)} %copy-done, f32[]{:T(128)} %bitcast.22, f32[]{:T(128)} %bitcast.18, f32[]{:T(128)S(6)} %mul.64), kind=kOutput, calls=%fused_computation | convolution fusion | flops 302743552 | bytes 3538956 | tf_op jit(solution)/shard_map/dot_general | solution.py:67
  125.4 0.0 collective-permute-done
  125.4 1.9 %convolution_add_fusion.1 = f32[256,1152]{1,0:T(8,128)} fusion(f32[256,1152]{1,0:T(8,128)S(1)} %fusion.16, bf16[256,1152]{1,0:T(8,128)(2,1)S(1)} %collective-permute-done, bf16[256,1152]{1,0:T(8,128)(2,1)S(1)} %copy-done.1, f32[]{:T(128)} %bitcast.20, f32[]{:T(128)} %bitcast.16, f32[]{:T(128)S(6)} %mul.64), kind=kOutput, calls=%fused_computation.1 | convolution fusion | flops 302743552 | bytes 3538956 | tf_op jit(solution)/shard_map/dot_general | solution.py:39
  (1 shorter events, 0.0 us)
Async XLA Ops:
  7.2 56.4 %all-gather.5.cloned.1.call-start = ((), (), s32[]{:S(2)}) async-start(), calls=%async_computation.1 | async-start | bytes 5308416 | tf_op jit(solution)/shard_map/all_gather | solution.py:42
  7.9 107.3 %all-gather.3.cloned.1.call-start = ((), (), s32[]{:S(2)}) async-start(), calls=%async_computation | async-start | bytes 5308416 | tf_op jit(solution)/shard_map/all_gather | solution.py:41
  8.6 113.5 %collective-permute-start.1 = (bf16[256,1152]{1,0:T(8,128)(2,1)}, bf16[256,1152]{1,0:T(8,128)(2,1)S(1)}, u32[]{:S(2)}, u32[]{:S(2)}) collective-permute-start(bf16[256,1152]{1,0:T(8,128)(2,1)} %param.4), channel_id=1, source_target_pairs={{0,24},{8,0},{16,8},{24,16},{1,25},{9,1},{17,9},{25,17},{2,26},{10... | collective-permute-start | bytes 1769480 | tf_op jit(solution)/shard_map/ppermute | solution.py:9
  12.6 112.7 %collective-permute-start = (bf16[256,1152]{1,0:T(8,128)(2,1)}, bf16[256,1152]{1,0:T(8,128)(2,1)S(1)}, u32[]{:S(2)}, u32[]{:S(2)}) collective-permute-start(bf16[256,1152]{1,0:T(8,128)(2,1)} %param.5), channel_id=1, source_target_pairs={{0,8},{8,16},{16,24},{24,0},{1,9},{9,17},{17,25},{25,1},{2,10},{10... | collective-permute-start | bytes 1769480 | tf_op jit(solution)/shard_map/ppermute | solution.py:9
  63.6 51.6 %copy-start.1 = (bf16[256,1152]{1,0:T(8,128)(2,1)S(1)}, bf16[256,1152]{1,0:T(8,128)(2,1)}, u32[]{:S(2)}) copy-start(bf16[256,1152]{1,0:T(8,128)(2,1)} %param.4) | copy-start | bytes 1769476
  115.2 6.9 %copy-start = (bf16[256,1152]{1,0:T(8,128)(2,1)S(1)}, bf16[256,1152]{1,0:T(8,128)(2,1)}, u32[]{:S(2)}) copy-start(bf16[256,1152]{1,0:T(8,128)(2,1)} %param.5) | copy-start | bytes 1769476
Sparse Core Ops, SparseCore 0:
  9.6 53.9 all-gather.4
  65.2 49.9 all-gather.2
where the time goes:
time: 134 us
  waiting for transfers between devices  94.6 us (71%)
  matrix products  20.1 us (15%)
  between operations  15.4 us (11%)
  starting transfers between devices  4.05 us (3%)
    all_gather x1, waiting for transfers between devices, shards(): lax.all_gather(picture_embedding_matrix, 'member', axis=0, tiled=True)  49.6 us
    all_gather x1, waiting for transfers between devices, shards(): lax.all_gather(caption_embedding_matrix, 'member', axis=0, tiled=True)  43.6 us
    dot_general x1, matrix products, shards(): jnp.dot(text_coeffs, group_img, preferred_element_type=jnp.float32)  8.07 us
    dot_general x1, matrix products, shards(): jnp.dot(score_multipliers, group_text_rows, preferred_element_type=jnp.fl...  6.88 us
    ppermute x2, starting transfers between devices, passed_along(): lax.ppermute(shard, axis, [(i, (i + by) % devices) for i in range(devices)])  3.98 us
    dot_general x1, matrix products, shards(): jnp.dot(next_coeffs, img_next, preferred_element_type=jnp.float32)  3.22 us
  transfers between devices with their start and end apart: 4, of which 2 were waited for; matrix products, arithmetic and copies ran while one was open for 14% of the time, Pallas kernels for 0%

commit v1 on v0

--- a/solution.py
+++ b/solution.py
@@ -39,7 +39,12 @@
     grad_prev = jnp.dot(earlier_multipliers, txt_prev, preferred_element_type=jnp.float32)
     group_text_rows, group_img = (
         lax.all_gather(caption_embedding_matrix, "member", axis=0, tiled=True),
-        lax.all_gather(picture_embedding_matrix, "member", axis=0, tiled=True),
+        jnp.concatenate(
+            lax.all_to_all(
+                jnp.stack([picture_embedding_matrix] * lax.axis_size("member")), "member", 0, 0
+            ),
+            axis=0,
+        ),
     )
     similarity_scores = (
         sharpness_multiplier

time: 134 us -> 188 us (1.40)
  waiting for transfers between devices: 94.6 us -> 139 us
  starting transfers between devices: 4.05 us -> 9.02 us
  local copies, waits for them, and re-layouts: 0.01 us -> 3.9 us
    all_to_all x0 -> x1, waiting for transfers between devices: none -> 139 us  [shards(): lax.all_to_all(jnp.stack([picture_embedding_matrix] * lax.axis_size('memb...]
    all_gather x1 -> x0, waiting for transfers between devices: 49.6 us -> none  [shards(): lax.all_gather(picture_embedding_matrix, 'member', axis=0, tiled=True)]
    all_gather x1, waiting for transfers between devices: 43.6 us -> 0.01 us  [shards(): lax.all_gather(caption_embedding_matrix, 'member', axis=0, tiled=True)]
    all_to_all x0 -> x1, starting transfers between devices: none -> 6.49 us  [shards(): lax.all_to_all(jnp.stack([picture_embedding_matrix] * lax.axis_size('memb...]
    another operation x0 -> x1, local copies, waits for them, and re-layouts: none -> 3.89 us  [shards(): jnp.stack([picture_embedding_matrix] * lax.axis_size('member'))]
  transfers between devices with their start and end apart: 4 -> 4, of which waited for: 2 -> 1; matrix products, arithmetic and copies ran while one was open for 14% -> 10% of each run, Pallas kernels for 0% -> 0%
where the time goes in v1:
time: 188 us
  waiting for transfers between devices  139 us (74%)
  matrix products  19.9 us (11%)
  between operations  15.4 us (8%)
  starting transfers between devices  9.02 us (5%)
  local copies, waits for them, and re-layouts  3.9 us (2%)
    all_to_all x1, waiting for transfers between devices, shards(): lax.all_to_all(jnp.stack([picture_embedding_matrix] * lax.axis_size('memb...  139 us
    dot_general x1, matrix products, shards(): jnp.dot(text_coeffs, group_img, preferred_element_type=jnp.float32)  7.86 us
    dot_general x1, matrix products, shards(): jnp.dot(score_multipliers, group_text_rows, preferred_element_type=jnp.fl...  6.84 us
    all_to_all x1, starting transfers between devices, shards(): lax.all_to_all(jnp.stack([picture_embedding_matrix] * lax.axis_size('memb...  6.49 us
    another operation x1, local copies, waits for them, and re-layouts, shards(): jnp.stack([picture_embedding_matrix] * lax.axis_size('member'))  3.89 us
  transfers between devices with their start and end apart: 4, of which 1 were waited for; matrix products, arithmetic and copies ran while one was open for 10% of the time, Pallas kernels for 0%

profile of v1, /device:TPU:0, one launch (start us, length us, event | category | flops | bytes accessed | tf_op | source)
XLA Modules:
  0.0 187.5 jit_solution(11321508338770350572)
XLA Ops:
  7.2 3.9 %stack.2 = bf16[8,256,1152]{2,1,0:T(8,128)(2,1)} broadcast(bf16[256,1152]{1,0:T(8,128)(2,1)} %param.4), dimensions={1,2} | broadcast | bytes 5308416 | tf_op jit(solution)/shard_map/stack | solution.py:44
  11.1 0.0 copy-start.1
  11.1 0.0 copy-start
  11.1 6.5 %all-to-all-start = ((bf16[8,256,1152]{2,1,0:T(8,128)(2,1)}), bf16[8,256,1152]{2,1,0:T(8,128)(2,1)}, u32[]{:S(2)}, u32[]{:S(2)}) async-start(bf16[8,256,1152]{2,1,0:T(8,128)(2,1)} %stack.2), calls=%async_computation | async-start | bytes 9437184 | tf_op jit(solution)/shard_map/all_to_all | solution.py:43
  17.5 0.0 all-gather.2.cloned.1.call-start
  17.6 0.7 all-gather.2.cloned.1.call-update
  18.3 0.0 copy-done.1
  18.3 2.5 %collective-permute-start.1 = (bf16[256,1152]{1,0:T(8,128)(2,1)S(1)}, bf16[256,1152]{1,0:T(8,128)(2,1)S(1)}, u32[]{:S(2)}, u32[]{:S(2)}) collective-permute-start(bf16[256,1152]{1,0:T(8,128)(2,1)S(1)} %copy-done.1), channel_id=1, source_target_pairs={{0,24},{8,0},{16,8},{24,16},{1,25},{9,1},{17,9},{25,17},{2,26},{10... | collective-permute-start | bytes 1769480 | tf_op jit(solution)/shard_map/ppermute | solution.py:9
  20.8 0.0 copy-done
  20.8 0.0 collective-permute-start
  22.1 138.7 %all-to-all-done = bf16[8,256,1152]{2,1,0:T(8,128)(2,1)} async-done(((bf16[8,256,1152]{2,1,0:T(8,128)(2,1)}), bf16[8,256,1152]{2,1,0:T(8,128)(2,1)}, u32[]{:S(2)}, u32[]{:S(2)}) %all-to-all-start) | async-done | bytes 4718624 | tf_op jit(solution)/shard_map/all_to_all | solution.py:43
  160.8 7.9 %fusion.17 = f32[256,1152]{1,0:T(8,128)} fusion(bf16[2048,1152]{1,0:T(8,128)(2,1)} %bitcast.2, bf16[256,1152]{1,0:T(8,128)(2,1)S(1)} %copy-done, f32[]{:T(128)} %bitcast.22, f32[]{:T(128)} %bitcast.18, s32[256]{0:T(256)S(1)} %iota_add_fusion, f32[]{:T(128)S(6)} %neg.22), kind=kOutput, calls=%fused_computation.24 | convolution fusion | flops 2422210560 | bytes 6489100 | tf_op jit(solution)/shard_map/dot_general | solution.py:71
  168.6 0.0 all-gather.2.cloned.1.call-done
  168.6 6.8 %fusion.16 = f32[256,1152]{1,0:T(8,128)S(1)} fusion(bf16[2048,1152]{1,0:T(8,128)(2,1)} %all-gather.2.cloned.1.call-done, bf16[256,1152]{1,0:T(8,128)(2,1)S(1)} %copy-done.1, f32[]{:T(128)} %bitcast.20, f32[]{:T(128)} %bitcast.16, s32[256]{0:T(256)S(1)} %iota_add_fusion, f32[]{:T(128)S(6)} %neg.22), kind=kOutput, calls=%fused_computation.23 | convolution fusion | flops 2422210560 | bytes 6489100 | tf_op jit(solution)/shard_map/dot_general | solution.py:56
  175.5 0.0 collective-permute-done.1
  175.5 3.2 %convolution_add_fusion = f32[256,1152]{1,0:T(8,128)} fusion(f32[256,1152]{1,0:T(8,128)} %fusion.17, bf16[256,1152]{1,0:T(8,128)(2,1)S(1)} %collective-permute-done.1, bf16[256,1152]{1,0:T(8,128)(2,1)S(1)} %copy-done, f32[]{:T(128)} %bitcast.23, f32[]{:T(128)} %bitcast.19, f32[]{:T(128)S(6)} %mul.64), kind=kOutput, calls=%fused_computation | convolution fusion | flops 302743552 | bytes 3538956 | tf_op jit(solution)/shard_map/dot_general | solution.py:72
  178.7 0.0 collective-permute-done
  178.7 1.9 %convolution_add_fusion.1 = f32[256,1152]{1,0:T(8,128)} fusion(f32[256,1152]{1,0:T(8,128)S(1)} %fusion.16, bf16[256,1152]{1,0:T(8,128)(2,1)S(1)} %collective-permute-done, bf16[256,1152]{1,0:T(8,128)(2,1)S(1)} %copy-done.1, f32[]{:T(128)} %bitcast.21, f32[]{:T(128)} %bitcast.17, f32[]{:T(128)S(6)} %mul.64), kind=kOutput, calls=%fused_computation.1 | convolution fusion | flops 302743552 | bytes 3538956 | tf_op jit(solution)/shard_map/dot_general | solution.py:39
  (1 shorter events, 0.0 us)
Async XLA Ops:
  11.1 7.2 %copy-start.1 = (bf16[256,1152]{1,0:T(8,128)(2,1)S(1)}, bf16[256,1152]{1,0:T(8,128)(2,1)}, u32[]{:S(2)}) copy-start(bf16[256,1152]{1,0:T(8,128)(2,1)} %param.4) | copy-start | bytes 1769476
  11.1 9.7 %copy-start = (bf16[256,1152]{1,0:T(8,128)(2,1)S(1)}, bf16[256,1152]{1,0:T(8,128)(2,1)}, u32[]{:S(2)}) copy-start(bf16[256,1152]{1,0:T(8,128)(2,1)} %param.5) | copy-start | bytes 1769476
  11.1 149.7 %all-to-all-start = ((bf16[8,256,1152]{2,1,0:T(8,128)(2,1)}), bf16[8,256,1152]{2,1,0:T(8,128)(2,1)}, u32[]{:S(2)}, u32[]{:S(2)}) async-start(bf16[8,256,1152]{2,1,0:T(8,128)(2,1)} %stack.2), calls=%async_computation | async-start | bytes 9437184 | tf_op jit(solution)/shard_map/all_to_all | solution.py:43
  17.5 151.1 %all-gather.2.cloned.1.call-start = ((), (), s32[]{:S(2)}) async-start(), calls=%async_computation.1 | async-start | bytes 5308416 | tf_op jit(solution)/shard_map/all_gather | solution.py:41
  18.3 157.2 %collective-permute-start.1 = (bf16[256,1152]{1,0:T(8,128)(2,1)S(1)}, bf16[256,1152]{1,0:T(8,128)(2,1)S(1)}, u32[]{:S(2)}, u32[]{:S(2)}) collective-permute-start(bf16[256,1152]{1,0:T(8,128)(2,1)S(1)} %copy-done.1), channel_id=1, source_target_pairs={{0,24},{8,0},{16,8},{24,16},{1,25},{9,1},{17,9},{25,17},{2,26},{10... | collective-permute-start | bytes 1769480 | tf_op jit(solution)/shard_map/ppermute | solution.py:9
  20.8 157.9 %collective-permute-start = (bf16[256,1152]{1,0:T(8,128)(2,1)S(1)}, bf16[256,1152]{1,0:T(8,128)(2,1)S(1)}, u32[]{:S(2)}, u32[]{:S(2)}) collective-permute-start(bf16[256,1152]{1,0:T(8,128)(2,1)S(1)} %copy-done), channel_id=1, source_target_pairs={{0,8},{8,16},{16,24},{24,0},{1,9},{9,17},{17,25},{25,1},{2,10},{10... | collective-permute-start | bytes 1769480 | tf_op jit(solution)/shard_map/ppermute | solution.py:9
Sparse Core Ops, SparseCore 0:
  20.0 90.0 all-gather.1
